TPU v7x, 32 devices: a whole 2x2x4 slice. The times are simulated.
32 devices in a mesh: groups: 2 (over y), tm: 4 (over x, core), space: 4 (over z).
Axes of the slice: x: 2, y: 2, z: 4, core: 2. Of those that a mesh axis runs over, the one named last changes fastest.
Arguments:
- features: bfloat16 [8, 32, 128, 256], P(('groups', 'tm'), 'space'), parts along dimension 0, may hold values from -6 to 6
- pair_order: int32 [8], P(('groups', 'tm')), parts along dimension 0, may hold values 0 or 1
- flow_now: bfloat16 [8, 2, 32, 128], P(('groups', 'tm'), None, 'space'), parts along dimension 0, may hold values from -8 to 8
- targets: int32 [8, 2, 32, 128], P(('groups', 'tm'), None, 'space'), parts along dimension 0, may hold values from -4 to 4
- w_volume: bfloat16 [162, 128], replicated, may hold values from -0.5 to 0.5
- b_volume: float32 [128], replicated, may hold values from -3 to 3
- w_code: bfloat16 [3, 3, 128, 128], replicated, may hold values from -0.1875 to 0.1875
- b_code: float32 [128], replicated, may hold values from -3 to 3
- w_flow: bfloat16 [7, 7, 2, 128], replicated, may hold values from -0.625 to 0.625
- b_flow: float32 [128], replicated, may hold values from -3 to 3
- w_joint: bfloat16 [3, 3, 256, 128], replicated, may hold values from -0.125 to 0.125
- b_joint: float32 [128], replicated, may hold values from -3 to 3
- w_head: bfloat16 [128, 2], replicated, may hold values from -0.5 to 0.5
- b_head: float32 [2], replicated, may hold values from -3 to 3
Outputs:
- loss: float32 [2], P('groups'), parts along dimension 0
- flow_error: float32 [8, 2, 32, 128], P(('groups', 'tm'), None, 'space'), parts along dimension 0
- grad_w_volume: float32 [324, 128], P('groups'), parts along dimension 0
- grad_b_volume: float32 [256], P('groups'), parts along dimension 0
- grad_w_code: float32 [6, 3, 128, 128], P('groups'), parts along dimension 0
- grad_b_code: float32 [256], P('groups'), parts along dimension 0
- grad_w_flow: float32 [14, 7, 2, 128], P('groups'), parts along dimension 0
- grad_b_flow: float32 [256], P('groups'), parts along dimension 0
- grad_w_joint: float32 [6, 3, 256, 128], P('groups'), parts along dimension 0
- grad_b_joint: float32 [256], P('groups'), parts along dimension 0
- grad_w_head: float32 [256, 2], P('groups'), parts along dimension 0
- grad_b_head: float32 [4], P('groups'), parts along dimension 0
There are 2 independent parts, one for each index of `groups`. A program takes and returns all parts, laid end to end along the dimension named above; an argument that names none is the same for every part. Nothing has to cross between parts.
All inputs are finite; a program needn't handle non-finite values. No bound on the sum of `pair_order` on one device may be relied on, other than what follows from the above.
Results may differ from a plain program's by a relative error of at most 0.0032.
Values may be sent and summed in bfloat16 or wider, within the bound.
No kernel may reach another device: no remote copies, remote signals or barrier semaphores. Data moves between devices by JAX's collectives and lax.ppermute only.
A program may use at most 64 MiB of HBM per device.

v0:
```python
import jax
import jax.numpy as jnp
from jax import lax
from jax.sharding import PartitionSpec as P

RADIUS = 4
highest_precision = lax.Precision.HIGHEST


def extended_2(array, sides, width):
    for axis, dim in sides:
        devices, length = (lax.axis_size(axis), array.shape[dim])
        up = [(i, (i + 1) % devices) for i in range(devices - 1)]
        down = [(j, i) for i, j in up]
        last = lax.slice_in_dim(array, length - width, length, axis=dim)
        first = lax.slice_in_dim(array, 0, width, axis=dim)
        before = lax.ppermute(last, axis, up)
        after = lax.ppermute(first, axis, down)
        array = jnp.concatenate([before, array, after], axis=dim)
    return array


def shifted(block, axis, distance):
    devices = range(lax.axis_size(axis))
    route = [(i - distance, i) for i in devices if i - distance in devices]
    return lax.ppermute(block, axis, route)


def silu_slope(values):
    sigma = jax.nn.sigmoid(values)
    return sigma * (1.0 + values * (1.0 - sigma))


def correlate(own_tile, other_ext):
    n_rows = own_tile.shape[0]
    n_cols = own_tile.shape[1]
    n_chan = own_tile.shape[2]
    side = 2 * RADIUS + 1
    padded_other = jnp.pad(other_ext, ((0, 0), (RADIUS, RADIUS), (0, 0)))
    bands = []
    for row_off in range(side):
        window = padded_other[row_off : row_off + n_rows]
        scores = jnp.einsum("rxc,ryc->rxy", own_tile, window, preferred_element_type=jnp.float32)
        flat_scores = scores.reshape(n_rows, n_cols * (n_cols + 2 * RADIUS))
        flat_scores = jnp.pad(flat_scores, ((0, 0), (0, n_cols)))
        bands.append(flat_scores.reshape(n_rows, n_cols, n_cols + side)[:, :, :side])
    stacked = jnp.stack(bands, axis=2).reshape(n_rows, n_cols, side * side)
    return (stacked * n_chan ** (-0.5)).astype(jnp.bfloat16)


def column_stack(extended, ksize):
    half_k = ksize // 2
    n_cols = extended.shape[1]
    padded = jnp.pad(extended, ((0, 0), (half_k, half_k), (0, 0)))
    return jnp.concatenate([padded[:, j : j + n_cols] for j in range(ksize)], axis=-1)


def conv_tile(extended, weight):
    ksize = weight.shape[0]
    half_k = ksize // 2
    n_rows = extended.shape[0] - 2 * half_k
    n_cols = extended.shape[1]
    stacked = column_stack(extended, ksize)
    depth = stacked.shape[2]
    summed = jnp.zeros((n_rows * n_cols, weight.shape[3]), jnp.float32)
    for i in range(ksize):
        taken = stacked[i : i + n_rows].reshape(n_rows * n_cols, depth)
        summed = summed + jnp.dot(
            taken, weight[i].reshape(depth, weight.shape[3]), preferred_element_type=jnp.float32
        )
    return summed


def conv_tile_back(extended_slope, weight):
    ksize = weight.shape[0]
    half_k = ksize // 2
    n_rows = extended_slope.shape[0] - 2 * half_k
    n_cols = extended_slope.shape[1]
    stacked = column_stack(extended_slope, ksize)
    depth = stacked.shape[2]
    summed = jnp.zeros((n_rows * n_cols, weight.shape[2]), jnp.float32)
    for row_at in range(ksize):
        i = ksize - 1 - row_at
        taken = stacked[row_at : row_at + n_rows].reshape(n_rows * n_cols, depth)
        w_rows = jnp.concatenate([weight[i, ksize - 1 - col_at] for col_at in range(ksize)], axis=1)
        summed = summed + lax.dot_general(
            taken, w_rows, (((1,), (1,)), ((), ())), preferred_element_type=jnp.float32
        )
    return summed


def conv_tile_grad(extended, slope_flat, ksize):
    half_k = ksize // 2
    n_rows = extended.shape[0] - 2 * half_k
    n_cols = extended.shape[1]
    stacked = column_stack(extended, ksize)
    depth = stacked.shape[2]
    taps = []
    for i in range(ksize):
        taken = stacked[i : i + n_rows].reshape(n_rows * n_cols, depth)
        rows_grad = lax.dot_general(
            taken, slope_flat, (((0,), (0,)), ((), ())), preferred_element_type=jnp.float32
        )
        taps.append(rows_grad.reshape(ksize, extended.shape[2], slope_flat.shape[1]))
    return jnp.stack(taps, axis=0)


def local(
    features,
    pair_order,
    flow_now,
    targets,
    w_volume,
    b_volume,
    w_code,
    b_code,
    w_flow,
    b_flow,
    w_joint,
    b_joint,
    w_head,
    b_head,
):
    own_tile = features[0]
    n_rows = own_tile.shape[0]
    n_cols = own_tile.shape[1]
    n_pix = n_rows * n_cols
    n_code = w_code.shape[3]
    own_ext = extended_2(own_tile, (("space", 0),), RADIUS)
    next_ext = shifted(own_ext, "tm", -1)
    forward = correlate(own_tile, next_ext)
    prior_ext = shifted(own_ext, "tm", 1)
    backward = correlate(own_tile, prior_ext)
    swapped = pair_order[0] == 1
    first_half = jnp.where(swapped, backward, forward)
    second_half = jnp.where(swapped, forward, backward)
    volume = jnp.concatenate([first_half, second_half], axis=-1)
    volume_flat = volume.reshape(n_pix, volume.shape[2])
    code_pre = jnp.dot(volume_flat, w_volume, preferred_element_type=jnp.float32) + b_volume
    code = jax.nn.silu(code_pre).astype(jnp.bfloat16)
    code_ext = extended_2(code.reshape(n_rows, n_cols, n_code), (("space", 0),), 1)
    motion_pre = conv_tile(code_ext, w_code) + b_code
    motion = jax.nn.silu(motion_pre).astype(jnp.bfloat16)
    flow_ext = extended_2(flow_now[0], (("space", 1),), 3)
    padded_flow = jnp.pad(flow_ext, ((0, 0), (0, 0), (3, 3)))
    patch_list = []
    for i in range(7):
        for j in range(7):
            for comp in range(2):
                patch_list.append(padded_flow[comp, i : i + n_rows, j : j + n_cols].reshape(n_pix))
    patches = jnp.stack(patch_list, axis=0)
    flow_weight = w_flow.reshape(98, n_code)
    flow_pre = (
        lax.dot_general(
            patches, flow_weight, (((0,), (0,)), ((), ())), preferred_element_type=jnp.float32
        )
        + b_flow
    )
    flow_code = jax.nn.silu(flow_pre).astype(jnp.bfloat16)
    joint = jnp.concatenate([motion, flow_code], axis=-1)
    joint_ext = extended_2(joint.reshape(n_rows, n_cols, 2 * n_code), (("space", 0),), 1)
    hidden_pre = conv_tile(joint_ext, w_joint) + b_joint
    hidden = jax.nn.silu(hidden_pre).astype(jnp.bfloat16)
    pred = jnp.dot(hidden, w_head, preferred_element_type=jnp.float32) + b_head
    target_flat = targets[0].reshape(2, n_pix).T.astype(jnp.float32)
    error_flat = pred - target_flat
    flow_error = error_flat.T.reshape(1, 2, n_rows, n_cols)
    n_frames = lax.axis_size("tm")
    frame_at = lax.axis_index("tm").astype(jnp.float32)
    frame_weight = jnp.power(jnp.float32(0.25), (n_frames - 1 - frame_at) / (n_frames - 1))
    count = 2.0 * n_frames * n_rows * lax.axis_size("space") * n_cols
    loss_local = jnp.reshape(frame_weight * jnp.sum(error_flat * error_flat) / count, (1,))
    slope_pred = 2.0 * frame_weight * error_flat / count
    grad_w_head = jnp.dot(hidden.astype(jnp.float32).T, slope_pred, precision=highest_precision)
    grad_b_head = jnp.sum(slope_pred, axis=0)
    slope_hidden = (
        jnp.dot(slope_pred, w_head.astype(jnp.float32).T, precision=highest_precision)
        * silu_slope(hidden_pre)
    ).astype(jnp.bfloat16)
    grad_w_joint = conv_tile_grad(joint_ext, slope_hidden, 3)
    grad_b_joint = jnp.sum(slope_hidden.astype(jnp.float32), axis=0)
    slope_ext = extended_2(slope_hidden.reshape(n_rows, n_cols, n_code), (("space", 0),), 1)
    slope_joint = conv_tile_back(slope_ext, w_joint)
    slope_motion = (slope_joint[:, :n_code] * silu_slope(motion_pre)).astype(jnp.bfloat16)
    slope_flow = (slope_joint[:, n_code:] * silu_slope(flow_pre)).astype(jnp.bfloat16)
    grad_w_flow = jnp.dot(patches, slope_flow, preferred_element_type=jnp.float32).reshape(
        7, 7, 2, n_code
    )
    grad_b_flow = jnp.sum(slope_flow.astype(jnp.float32), axis=0)
    grad_w_code = conv_tile_grad(code_ext, slope_motion, 3)
    grad_b_code = jnp.sum(slope_motion.astype(jnp.float32), axis=0)
    motion_ext = extended_2(slope_motion.reshape(n_rows, n_cols, n_code), (("space", 0),), 1)
    slope_code = (conv_tile_back(motion_ext, w_code) * silu_slope(code_pre)).astype(jnp.bfloat16)
    grad_w_volume = lax.dot_general(
        volume_flat, slope_code, (((0,), (0,)), ((), ())), preferred_element_type=jnp.float32
    )
    grad_b_volume = jnp.sum(slope_code.astype(jnp.float32), axis=0)
    (
        loss_local,
        grad_w_volume,
        grad_b_volume,
        grad_w_code,
        grad_b_code,
        grad_w_flow,
        grad_b_flow,
        grad_w_joint,
        grad_b_joint,
        grad_w_head,
        grad_b_head,
    ) = lax.psum(
        (
            loss_local,
            grad_w_volume,
            grad_b_volume,
            grad_w_code,
            grad_b_code,
            grad_w_flow,
            grad_b_flow,
            grad_w_joint,
            grad_b_joint,
            grad_w_head,
            grad_b_head,
        ),
        ("tm", "space"),
    )
    return (
        loss_local,
        flow_error,
        grad_w_volume,
        grad_b_volume,
        grad_w_code,
        grad_b_code,
        grad_w_flow,
        grad_b_flow,
        grad_w_joint,
        grad_b_joint,
        grad_w_head,
        grad_b_head,
    )


def solution(mesh):
    placed = (
        P(("groups", "tm"), "space", None, None),
        P(("groups", "tm")),
        P(("groups", "tm"), None, "space", None),
        P(("groups", "tm"), None, "space", None),
        P(),
        P(),
        P(),
        P(),
        P(),
        P(),
        P(),
        P(),
        P(),
        P(),
    )
    return jax.shard_map(
        local,
        mesh=mesh,
        in_specs=placed,
        out_specs=(
            P("groups"),
            P(("groups", "tm"), None, "space", None),
            P("groups", None),
            P("groups"),
            P("groups", None, None, None),
            P("groups"),
            P("groups", None, None, None),
            P("groups"),
            P("groups", None, None, None),
            P("groups"),
            P("groups", None),
            P("groups"),
        ),
        check_vma=False,
    )
```

profile of v0, /device:TPU:0, one launch (start us, length us, event | category | flops | bytes accessed | tf_op | source)
XLA Modules:
  0.0 301.7 jit_solution(11512304857704696042)
XLA Ops:
  8.4 4.9 %collective-permute-start = (bf16[4,128,256]{2,1,0:T(8,128)(2,1)S(1)}, bf16[4,128,256]{2,1,0:T(8,128)(2,1)S(1)}, u32[]{:S(2)}, u32[]{:S(2)}) collective-permute-start(bf16[4,128,256]{2,1,0:T(8,128)(2,1)S(1)} %get-tuple-element.61), channel_id=1, source_target_pairs={{0,1},{1,2},{2,3},{4,5},{5,6},{6,7},{8,9},{9,10},{10,11},{12,13},{... | collective-permute-start | bytes 786440 | tf_op jit(solution)/shard_map/ppermute | solution.py:17
  15.4 4.5 %collective-permute-start.6 = (bf16[2,3,128]{2,1,0:T(4,128)(2,1)S(1)}, bf16[2,3,128]{2,1,0:T(4,128)(2,1)S(1)}, u32[]{:S(2)}, u32[]{:S(2)}) collective-permute-start(bf16[2,3,128]{2,1,0:T(4,128)(2,1)S(1)} %get-tuple-element.186), channel_id=1, source_target_pairs={{0,1},{1,2},{2,3},{4,5},{5,6},{6,7},{8,9},{9,10},{10,11},{12,13},{... | collective-permute-start | bytes 4616 | tf_op jit(solution)/shard_map/ppermute | solution.py:17
  22.0 2.0 fusion.158
  32.2 4.2 %collective-permute-start.2 = (bf16[16,128,256]{2,1,0:T(8,128)(2,1)}, bf16[16,128,256]{2,1,0:T(8,128)(2,1)}, u32[]{:S(2)}, u32[]{:S(2)}) collective-permute-start(bf16[16,128,256]{2,1,0:T(8,128)(2,1)} %pad_maximum_fusion.2), channel_id=1, source_target_pairs={{0,4},{4,8},{8,12},{1,5},{5,9},{9,13},{2,6},{6,10},{10,14},{3,7},{... | collective-permute-start | bytes 3145736 | tf_op jit(solution)/shard_map/ppermute | solution.py:26
  41.1 1.4 convolution_bitcast_fusion.7
  44.8 1.4 convolution_bitcast_fusion.6
  48.5 1.4 convolution_bitcast_fusion.5
  52.2 1.4 convolution_bitcast_fusion.4
  55.9 1.8 convolution_bitcast_fusion.3
  60.7 1.4 convolution_bitcast_fusion.2
  69.9 1.4 convolution_bitcast_fusion.17
  73.6 1.4 convolution_bitcast_fusion.16
  99.7 1.4 convolution_bitcast_fusion.10
  114.4 4.5 %collective-permute-start.4 = (bf16[1,128,128]{2,1,0:T(8,128)(2,1)S(1)}, bf16[1,128,128]{2,1,0:T(8,128)(2,1)S(1)}, u32[]{:S(2)}, u32[]{:S(2)}) collective-permute-start(bf16[1,128,128]{2,1,0:T(8,128)(2,1)S(1)} %get-tuple-element.85), channel_id=1, source_target_pairs={{0,1},{1,2},{2,3},{4,5},{5,6},{6,7},{8,9},{9,10},{10,11},{12,13},{... | collective-permute-start | bytes 98312 | tf_op jit(solution)/shard_map/ppermute | solution.py:17
  121.3 3.4 %collective-permute-done.5 = bf16[1,128,128]{2,1,0:T(8,128)(2,1)S(1)} collective-permute-done((bf16[1,128,128]{2,1,0:T(8,128)(2,1)S(1)}, bf16[1,128,128]{2,1,0:T(8,128)(2,1)S(1)}, u32[]{:S(2)}, u32[]{:S(2)}) %collective-permute-start.5) | collective-permute-done | bytes 32800 | tf_op jit(solution)/shard_map/ppermute | solution.py:18
  132.0 3.5 %collective-permute-start.8 = (bf16[1,128,256]{2,1,0:T(8,128)(2,1)S(1)}, bf16[1,128,256]{2,1,0:T(8,128)(2,1)S(1)}, u32[]{:S(2)}, u32[]{:S(2)}) collective-permute-start(bf16[1,128,256]{2,1,0:T(8,128)(2,1)S(1)} %get-tuple-element.59), channel_id=1, source_target_pairs={{0,1},{1,2},{2,3},{4,5},{5,6},{6,7},{8,9},{9,10},{10,11},{12,13},{... | collective-permute-start | bytes 196616 | tf_op jit(solution)/shard_map/ppermute | solution.py:17
  135.5 1.5 collective-permute-start.9
  137.4 4.3 %collective-permute-done.9 = bf16[1,128,256]{2,1,0:T(8,128)(2,1)S(1)} collective-permute-done((bf16[1,128,256]{2,1,0:T(8,128)(2,1)S(1)}, bf16[1,128,256]{2,1,0:T(8,128)(2,1)S(1)}, u32[]{:S(2)}, u32[]{:S(2)}) %collective-permute-start.9) | collective-permute-done | bytes 65568 | tf_op jit(solution)/shard_map/ppermute | solution.py:18
  142.2 1.7 fusion.153
  143.9 1.6 copy.98
  145.5 2.4 fusion.165
  148.7 2.3 fusion.166
  151.0 1.7 copy.97
  152.7 2.4 multiply_convert_fusion
  159.1 3.5 %collective-permute-start.10 = (bf16[1,128,128]{2,1,0:T(8,128)(2,1)S(1)}, bf16[1,128,128]{2,1,0:T(8,128)(2,1)S(1)}, u32[]{:S(2)}, u32[]{:S(2)}) collective-permute-start(bf16[1,128,128]{2,1,0:T(8,128)(2,1)S(1)} %get-tuple-element.83), channel_id=1, source_target_pairs={{0,1},{1,2},{2,3},{4,5},{5,6},{6,7},{8,9},{9,10},{10,11},{12,13},{... | collective-permute-start | bytes 98312 | tf_op jit(solution)/shard_map/ppermute | solution.py:17
  165.0 3.4 %collective-permute-done.11 = bf16[1,128,128]{2,1,0:T(8,128)(2,1)S(1)} collective-permute-done((bf16[1,128,128]{2,1,0:T(8,128)(2,1)S(1)}, bf16[1,128,128]{2,1,0:T(8,128)(2,1)S(1)}, u32[]{:S(2)}, u32[]{:S(2)}) %collective-permute-start.11) | collective-permute-done | bytes 32800 | tf_op jit(solution)/shard_map/ppermute | solution.py:18
  174.0 1.9 collective-permute-start.12
  178.1 3.6 %collective-permute-done.13 = bf16[1,128,128]{2,1,0:T(8,128)(2,1)S(1)} collective-permute-done((bf16[1,128,128]{2,1,0:T(8,128)(2,1)S(1)}, bf16[1,128,128]{2,1,0:T(8,128)(2,1)S(1)}, u32[]{:S(2)}, u32[]{:S(2)}) %collective-permute-start.13) | collective-permute-done | bytes 32800 | tf_op jit(solution)/shard_map/ppermute | solution.py:18
  187.7 62.3 %all-reduce.25 = (f32[1]{0:T(128)}, f32[128]{0:T(128)}, f32[128]{0:T(128)}, f32[7,7,2,128]{3,2,1,0:T(2,128)}, f32[128]{0:T(128)}, /*index=5*/f32[128]{0:T(128)}, f32[128,2]{0,1:T(2,128)}, f32[2]{0:T(128)}) all-reduce(f32[1]{0:T(128)} %bitcast.60, ...), channel_id=1, replica_groups=mesh['groups'=2,'tm'=4,'space'=4] {'tm','space'}, use_global_device_ids=true, to_apply=%region_1.2 | all-reduce | flops 13315 | bytes 106520 | tf_op jit(solution)/shard_map/psum | solution.py:210
  250.0 39.9 %all-reduce.29.cloned.1.call-done = (f32[162,128]{1,0:T(8,128)}, f32[3,3,128,128]{3,2,1,0:T(8,128)}, f32[3,3,256,128]{3,2,1,0:T(8,128)}) async-done(((f32[162,128]{1,0:T(8,128)}, f32[3,3,128,128]{3,2,1,0:T(8,128)}, f32[3,3,256,128]{3,2,1,0:T(8,128)}), (f32[162,128]{1,0:T(8,128)}, f32[3,3,128,128]{3,2,1,0:T(8,128)}, f32[3,3,256,128]{3,2,1,0:T(8,128)})) %all-reduce.29.cloned.1.call-update) | async-done | bytes 1852432 | tf_op jit(solution)/shard_map/psum | solution.py:210
  289.9 1.6 copy.329
  291.5 1.9 copy.330
  (397 shorter events, 107.7 us)
Async XLA Ops:
  7.2 105.9 %copy-start = (bf16[162,128]{1,0:T(8,128)(2,1)S(1)}, bf16[162,128]{1,0:T(8,128)(2,1)}, u32[]{:S(2)}) copy-start(bf16[162,128]{1,0:T(8,128)(2,1)} %param.18) | copy-start | bytes 124420
  7.2 16.8 %copy-start.5 = (bf16[3,3,256,128]{3,2,1,0:T(8,128)(2,1)S(1)}, bf16[3,3,256,128]{3,2,1,0:T(8,128)(2,1)}, u32[]{:S(2)}) copy-start(bf16[3,3,256,128]{3,2,1,0:T(8,128)(2,1)} %param.24) | copy-start | bytes 1769476
  7.2 17.6 %copy-start.8 = (bf16[3,3,128,128]{3,2,1,0:T(8,128)(2,1)S(1)}, bf16[3,3,128,128]{3,2,1,0:T(8,128)(2,1)}, u32[]{:S(2)}) copy-start(bf16[3,3,128,128]{3,2,1,0:T(8,128)(2,1)} %param.20) | copy-start | bytes 884740
  7.2 282.6 %all-reduce.29.cloned.1.call-start = ((), (), s32[]{:S(2)}) async-start(), calls=%async_computation | async-start | bytes 3710976 | tf_op jit(solution)/shard_map/psum | solution.py:210
  8.4 20.4 %collective-permute-start = (bf16[4,128,256]{2,1,0:T(8,128)(2,1)S(1)}, bf16[4,128,256]{2,1,0:T(8,128)(2,1)S(1)}, u32[]{:S(2)}, u32[]{:S(2)}) collective-permute-start(bf16[4,128,256]{2,1,0:T(8,128)(2,1)S(1)} %get-tuple-element.61), channel_id=1, source_target_pairs={{0,1},{1,2},{2,3},{4,5},{5,6},{6,7},{8,9},{9,10},{10,11},{12,13},{... | collective-permute-start | bytes 786440 | tf_op jit(solution)/shard_map/ppermute | solution.py:17
  13.4 15.5 %collective-permute-start.1 = (bf16[4,128,256]{2,1,0:T(8,128)(2,1)S(1)}, bf16[4,128,256]{2,1,0:T(8,128)(2,1)S(1)}, u32[]{:S(2)}, u32[]{:S(2)}) collective-permute-start(bf16[4,128,256]{2,1,0:T(8,128)(2,1)S(1)} %get-tuple-element.62), channel_id=1, source_target_pairs={{1,0},{2,1},{3,2},{5,4},{6,5},{7,6},{9,8},{10,9},{11,10},{13,12},{... | collective-permute-start | bytes 786440 | tf_op jit(solution)/shard_map/ppermute | solution.py:18
  15.4 12.1 %collective-permute-start.6 = (bf16[2,3,128]{2,1,0:T(4,128)(2,1)S(1)}, bf16[2,3,128]{2,1,0:T(4,128)(2,1)S(1)}, u32[]{:S(2)}, u32[]{:S(2)}) collective-permute-start(bf16[2,3,128]{2,1,0:T(4,128)(2,1)S(1)} %get-tuple-element.186), channel_id=1, source_target_pairs={{0,1},{1,2},{2,3},{4,5},{5,6},{6,7},{8,9},{9,10},{10,11},{12,13},{... | collective-permute-start | bytes 4616 | tf_op jit(solution)/shard_map/ppermute | solution.py:17
  20.0 7.6 %collective-permute-start.7 = (bf16[2,3,128]{2,1,0:T(4,128)(2,1)S(1)}, bf16[2,3,128]{2,1,0:T(4,128)(2,1)S(1)}, u32[]{:S(2)}, u32[]{:S(2)}) collective-permute-start(bf16[2,3,128]{2,1,0:T(4,128)(2,1)S(1)} %get-tuple-element.187), channel_id=1, source_target_pairs={{1,0},{2,1},{3,2},{5,4},{6,5},{7,6},{9,8},{10,9},{11,10},{13,12},{... | collective-permute-start | bytes 4616 | tf_op jit(solution)/shard_map/ppermute | solution.py:18
  22.0 4.2 %copy-start.51 = (s32[1,2,8,128]{3,2,1,0:T(8,128)S(1)}, s32[1,2,8,128]{3,2,1,0:T(8,128)}, u32[]{:S(2)}) copy-start(s32[1,2,8,128]{3,2,1,0:T(8,128)} %param.17) | copy-start | bytes 24580
  22.0 4.9 %copy-start.50 = (bf16[7,7,2,128]{3,2,1,0:T(2,128)(2,1)S(1)}, bf16[7,7,2,128]{3,2,1,0:T(2,128)(2,1)}, u32[]{:S(2)}) copy-start(bf16[7,7,2,128]{3,2,1,0:T(2,128)(2,1)} %param.22) | copy-start | bytes 75268
  22.0 5.6 %copy-start.44 = (bf16[1,2,8,128]{3,2,1,0:T(8,128)(2,1)S(1)}, bf16[1,2,8,128]{3,2,1,0:T(8,128)(2,1)}, u32[]{:S(2)}) copy-start(bf16[1,2,8,128]{3,2,1,0:T(8,128)(2,1)} %param.16) | copy-start | bytes 12292
  24.0 4.9 %copy-start.6 = (bf16[1,8,128,256]{3,2,1,0:T(8,128)(2,1)S(1)}, bf16[1,8,128,256]{3,2,1,0:T(8,128)(2,1)}, u32[]{:S(2)}) copy-start(bf16[1,8,128,256]{3,2,1,0:T(8,128)(2,1)} %param.14) | copy-start | bytes 1572868
  29.9 6.5 %collective-permute-start.3 = (bf16[16,128,256]{2,1,0:T(8,128)(2,1)}, bf16[16,128,256]{2,1,0:T(8,128)(2,1)S(1)}, u32[]{:S(2)}, u32[]{:S(2)}) collective-permute-start(bf16[16,128,256]{2,1,0:T(8,128)(2,1)} %pad_maximum_fusion.2), channel_id=1, source_target_pairs={{4,0},{8,4},{12,8},{5,1},{9,5},{13,9},{6,2},{10,6},{14,10},{7,3},{... | collective-permute-start | bytes 3145736 | tf_op jit(solution)/shard_map/ppermute | solution.py:26
  32.2 37.7 %collective-permute-start.2 = (bf16[16,128,256]{2,1,0:T(8,128)(2,1)}, bf16[16,128,256]{2,1,0:T(8,128)(2,1)}, u32[]{:S(2)}, u32[]{:S(2)}) collective-permute-start(bf16[16,128,256]{2,1,0:T(8,128)(2,1)} %pad_maximum_fusion.2), channel_id=1, source_target_pairs={{0,4},{4,8},{8,12},{1,5},{5,9},{9,13},{2,6},{6,10},{10,14},{3,7},{... | collective-permute-start | bytes 3145736 | tf_op jit(solution)/shard_map/ppermute | solution.py:26
  110.8 1.6 copy-start.30
  110.9 1.6 copy-start.31
  110.9 1.6 copy-start.32
  113.1 7.1 %copy-start.49 = (bf16[98,128]{1,0:T(8,128)(2,1)S(1)}, bf16[98,128]{1,0:T(8,128)(2,1)}, u32[]{:S(2)}) copy-start(bf16[98,128]{1,0:T(8,128)(2,1)} %reshape.316) | copy-start | bytes 75268
  113.1 7.1 %copy-start.54 = (f32[128]{0:T(128)S(1)}, f32[128]{0:T(128)}, u32[]{:S(2)}) copy-start(f32[128]{0:T(128)} %param.23) | copy-start | bytes 1540
  114.4 7.0 %collective-permute-start.4 = (bf16[1,128,128]{2,1,0:T(8,128)(2,1)S(1)}, bf16[1,128,128]{2,1,0:T(8,128)(2,1)S(1)}, u32[]{:S(2)}, u32[]{:S(2)}) collective-permute-start(bf16[1,128,128]{2,1,0:T(8,128)(2,1)S(1)} %get-tuple-element.85), channel_id=1, source_target_pairs={{0,1},{1,2},{2,3},{4,5},{5,6},{6,7},{8,9},{9,10},{10,11},{12,13},{... | collective-permute-start | bytes 98312 | tf_op jit(solution)/shard_map/ppermute | solution.py:17
  118.9 5.8 %collective-permute-start.5 = (bf16[1,128,128]{2,1,0:T(8,128)(2,1)S(1)}, bf16[1,128,128]{2,1,0:T(8,128)(2,1)S(1)}, u32[]{:S(2)}, u32[]{:S(2)}) collective-permute-start(bf16[1,128,128]{2,1,0:T(8,128)(2,1)S(1)} %get-tuple-element.86), channel_id=1, source_target_pairs={{1,0},{2,1},{3,2},{5,4},{6,5},{7,6},{9,8},{10,9},{11,10},{13,12},{... | collective-permute-start | bytes 98312 | tf_op jit(solution)/shard_map/ppermute | solution.py:18
  132.0 5.4 %collective-permute-start.8 = (bf16[1,128,256]{2,1,0:T(8,128)(2,1)S(1)}, bf16[1,128,256]{2,1,0:T(8,128)(2,1)S(1)}, u32[]{:S(2)}, u32[]{:S(2)}) collective-permute-start(bf16[1,128,256]{2,1,0:T(8,128)(2,1)S(1)} %get-tuple-element.59), channel_id=1, source_target_pairs={{0,1},{1,2},{2,3},{4,5},{5,6},{6,7},{8,9},{9,10},{10,11},{12,13},{... | collective-permute-start | bytes 196616 | tf_op jit(solution)/shard_map/ppermute | solution.py:17
  135.5 6.2 %collective-permute-start.9 = (bf16[1,128,256]{2,1,0:T(8,128)(2,1)S(1)}, bf16[1,128,256]{2,1,0:T(8,128)(2,1)S(1)}, u32[]{:S(2)}, u32[]{:S(2)}) collective-permute-start(bf16[1,128,256]{2,1,0:T(8,128)(2,1)S(1)} %get-tuple-element.60), channel_id=1, source_target_pairs={{1,0},{2,1},{3,2},{5,4},{6,5},{7,6},{9,8},{10,9},{11,10},{13,12},{... | collective-permute-start | bytes 196616 | tf_op jit(solution)/shard_map/ppermute | solution.py:18
  151.0 1.7 copy-start.56
  152.7 2.4 copy-start.57
  152.7 2.4 copy-start.58
  159.1 5.9 %collective-permute-start.10 = (bf16[1,128,128]{2,1,0:T(8,128)(2,1)S(1)}, bf16[1,128,128]{2,1,0:T(8,128)(2,1)S(1)}, u32[]{:S(2)}, u32[]{:S(2)}) collective-permute-start(bf16[1,128,128]{2,1,0:T(8,128)(2,1)S(1)} %get-tuple-element.83), channel_id=1, source_target_pairs={{0,1},{1,2},{2,3},{4,5},{5,6},{6,7},{8,9},{9,10},{10,11},{12,13},{... | collective-permute-start | bytes 98312 | tf_op jit(solution)/shard_map/ppermute | solution.py:17
  162.6 5.8 %collective-permute-start.11 = (bf16[1,128,128]{2,1,0:T(8,128)(2,1)S(1)}, bf16[1,128,128]{2,1,0:T(8,128)(2,1)S(1)}, u32[]{:S(2)}, u32[]{:S(2)}) collective-permute-start(bf16[1,128,128]{2,1,0:T(8,128)(2,1)S(1)} %get-tuple-element.84), channel_id=1, source_target_pairs={{1,0},{2,1},{3,2},{5,4},{6,5},{7,6},{9,8},{10,9},{11,10},{13,12},{... | collective-permute-start | bytes 98312 | tf_op jit(solution)/shard_map/ppermute | solution.py:18
  174.0 4.1 %collective-permute-start.12 = (bf16[1,128,128]{2,1,0:T(8,128)(2,1)S(1)}, bf16[1,128,128]{2,1,0:T(8,128)(2,1)S(1)}, u32[]{:S(2)}, u32[]{:S(2)}) collective-permute-start(bf16[1,128,128]{2,1,0:T(8,128)(2,1)S(1)} %get-tuple-element.81), channel_id=1, source_target_pairs={{0,1},{1,2},{2,3},{4,5},{5,6},{6,7},{8,9},{9,10},{10,11},{12,13},{... | collective-permute-start | bytes 98312 | tf_op jit(solution)/shard_map/ppermute | solution.py:17
  176.0 5.8 %collective-permute-start.13 = (bf16[1,128,128]{2,1,0:T(8,128)(2,1)S(1)}, bf16[1,128,128]{2,1,0:T(8,128)(2,1)S(1)}, u32[]{:S(2)}, u32[]{:S(2)}) collective-permute-start(bf16[1,128,128]{2,1,0:T(8,128)(2,1)S(1)} %get-tuple-element.82), channel_id=1, source_target_pairs={{1,0},{2,1},{3,2},{5,4},{6,5},{7,6},{9,8},{10,9},{11,10},{13,12},{... | collective-permute-start | bytes 98312 | tf_op jit(solution)/shard_map/ppermute | solution.py:18
  184.5 2.7 copy-start.22
  289.9 3.5 %copy-start.7 = (f32[3,3,256,128]{3,2,1,0:T(8,128)S(1)}, f32[3,3,256,128]{3,2,1,0:T(8,128)}, u32[]{:S(2)}) copy-start(f32[3,3,256,128]{3,2,1,0:T(8,128)} %get-tuple-element.309) | copy-start | bytes 3538948
  (43 other events, 45.8 us)
Sparse Core Ops, SparseCore 0:
  186.1 103.6 all-reduce.28
where the time goes:
time: 306 us; the launch traced here: 302 us
  local copies, waits for them, and re-layouts  80 us (26%)
  blocking collectives  62.3 us (20%)
  waiting for transfers between devices  54.9 us (18%)
  matrix products  45.1 us (15%)
  starting transfers between devices  36.4 us (12%)
  between operations  18.2 us (6%)
  other arithmetic  4.82 us (2%)
    psum x1, blocking collectives, local(): lax.psum((loss_local, grad_w_volume, grad_b_volume, grad_w_code, grad_b_c...  62.3 us
    psum x1, waiting for transfers between devices, local(): lax.psum((loss_local, grad_w_volume, grad_b_volume, grad_w_code, grad_b_c...  39.9 us
    dot_general x18, matrix products, correlate(): jnp.einsum('rxc,ryc->rxy', own_tile, window, preferred_element_type=jnp.f...  24.8 us
    ppermute x6, starting transfers between devices, extended_2(): before = lax.ppermute(last, axis, up)  22.9 us
    reshape x18, local copies, waits for them, and re-layouts, correlate(): flat_scores.reshape(n_rows, n_cols, n_cols + side)[:, :, :side]  20.9 us
    ppermute x6, waiting for transfers between devices, extended_2(): after = lax.ppermute(first, axis, down)  14.7 us
    unnamed x150, local copies, waits for them, and re-layouts  12.4 us
    another operation x37, local copies, waits for them, and re-layouts, correlate(): stacked = jnp.stack(bands, axis=2).reshape(n_rows, n_cols, side * side)  10.8 us
  transfers between devices with their start and end apart: 15, of which 6 were waited for; matrix products, arithmetic and copies ran while one was open for 15% of the time, Pallas kernels for 0%

commit v1 on v0

--- a/solution.py
+++ b/solution.py
@@ -5,6 +5,11 @@
 
 RADIUS = 4
 highest_precision = lax.Precision.HIGHEST
+
+
+def recast_boxes_in(base_x):
+    z2 = lax.psum(lax.psum(base_x, axis_name="space"), "tm")
+    return z2
 
 
 def extended_2(array, sides, width):
@@ -207,7 +212,7 @@
         grad_b_joint,
         grad_w_head,
         grad_b_head,
-    ) = lax.psum(
+    ) = recast_boxes_in(
         (
             loss_local,
             grad_w_volume,
@@ -220,8 +225,7 @@
             grad_b_joint,
             grad_w_head,
             grad_b_head,
-        ),
-        ("tm", "space"),
+        )
     )
     return (
         loss_local,

time: 306 us -> 338 us (1.10)
  waiting for transfers between devices: 54.9 us -> 118 us
  blocking collectives: 62.3 us -> 30.9 us
    psum x1 -> x2, waiting for transfers between devices: 39.9 us -> 103 us  [recast_boxes_in(): z2 = lax.psum(lax.psum(base_x, axis_name='space'), 'tm')]
    psum x1 -> x2, blocking collectives: 62.3 us -> 30.9 us  [recast_boxes_in(): z2 = lax.psum(lax.psum(base_x, axis_name='space'), 'tm')]
  transfers between devices with their start and end apart: 15 -> 16, of which waited for: 6 -> 7; matrix products, arithmetic and copies ran while one was open for 15% -> 13% of each run, Pallas kernels for 0% -> 0%
where the time goes in v1:
time: 338 us; the launch traced here: 333 us
  waiting for transfers between devices  118 us (35%)
  local copies, waits for them, and re-layouts  80.1 us (24%)
  matrix products  45.1 us (13%)
  starting transfers between devices  36.5 us (11%)
  blocking collectives  30.9 us (9%)
  between operations  18.2 us (5%)
  other arithmetic  4.82 us (1%)
    psum x2, waiting for transfers between devices, recast_boxes_in(): z2 = lax.psum(lax.psum(base_x, axis_name='space'), 'tm')  103 us
    psum x2, blocking collectives, recast_boxes_in(): z2 = lax.psum(lax.psum(base_x, axis_name='space'), 'tm')  30.9 us
    dot_general x18, matrix products, correlate(): jnp.einsum('rxc,ryc->rxy', own_tile, window, preferred_element_type=jnp.f...  24.8 us
    ppermute x6, starting transfers between devices, extended_2(): before = lax.ppermute(last, axis, up)  22.9 us
    reshape x18, local copies, waits for them, and re-layouts, correlate(): flat_scores.reshape(n_rows, n_cols, n_cols + side)[:, :, :side]  20.9 us
    ppermute x6, waiting for transfers between devices, extended_2(): after = lax.ppermute(first, axis, down)  14.7 us
    unnamed x150, local copies, waits for them, and re-layouts  12.4 us
    another operation x37, local copies, waits for them, and re-layouts, correlate(): stacked = jnp.stack(bands, axis=2).reshape(n_rows, n_cols, side * side)  10.8 us
  transfers between devices with their start and end apart: 16, of which 7 were waited for; matrix products, arithmetic and copies ran while one was open for 13% of the time, Pallas kernels for 0%

profile of v1, /device:TPU:0, one launch (start us, length us, event | category | flops | bytes accessed | tf_op | source)
XLA Modules:
  0.0 333.5 jit_solution(13241918496857038073)
XLA Ops:
  8.4 4.9 %collective-permute-start = (bf16[4,128,256]{2,1,0:T(8,128)(2,1)S(1)}, bf16[4,128,256]{2,1,0:T(8,128)(2,1)S(1)}, u32[]{:S(2)}, u32[]{:S(2)}) collective-permute-start(bf16[4,128,256]{2,1,0:T(8,128)(2,1)S(1)} %get-tuple-element.72), channel_id=1, source_target_pairs={{0,1},{1,2},{2,3},{4,5},{5,6},{6,7},{8,9},{9,10},{10,11},{12,13},{... | collective-permute-start | bytes 786440 | tf_op jit(solution)/shard_map/ppermute | solution.py:22
  15.4 4.5 %collective-permute-start.6 = (bf16[2,3,128]{2,1,0:T(4,128)(2,1)S(1)}, bf16[2,3,128]{2,1,0:T(4,128)(2,1)S(1)}, u32[]{:S(2)}, u32[]{:S(2)}) collective-permute-start(bf16[2,3,128]{2,1,0:T(4,128)(2,1)S(1)} %get-tuple-element.197), channel_id=1, source_target_pairs={{0,1},{1,2},{2,3},{4,5},{5,6},{6,7},{8,9},{9,10},{10,11},{12,13},{... | collective-permute-start | bytes 4616 | tf_op jit(solution)/shard_map/ppermute | solution.py:22
  22.0 2.0 fusion.158
  32.2 4.2 %collective-permute-start.2 = (bf16[16,128,256]{2,1,0:T(8,128)(2,1)}, bf16[16,128,256]{2,1,0:T(8,128)(2,1)}, u32[]{:S(2)}, u32[]{:S(2)}) collective-permute-start(bf16[16,128,256]{2,1,0:T(8,128)(2,1)} %pad_maximum_fusion.2), channel_id=1, source_target_pairs={{0,4},{4,8},{8,12},{1,5},{5,9},{9,13},{2,6},{6,10},{10,14},{3,7},{... | collective-permute-start | bytes 3145736 | tf_op jit(solution)/shard_map/ppermute | solution.py:31
  41.1 1.4 convolution_bitcast_fusion.7
  44.8 1.4 convolution_bitcast_fusion.6
  48.5 1.4 convolution_bitcast_fusion.5
  52.2 1.4 convolution_bitcast_fusion.4
  55.9 1.8 convolution_bitcast_fusion.3
  69.9 1.4 convolution_bitcast_fusion.17
  73.6 1.4 convolution_bitcast_fusion.16
  114.4 4.5 %collective-permute-start.4 = (bf16[1,128,128]{2,1,0:T(8,128)(2,1)S(1)}, bf16[1,128,128]{2,1,0:T(8,128)(2,1)S(1)}, u32[]{:S(2)}, u32[]{:S(2)}) collective-permute-start(bf16[1,128,128]{2,1,0:T(8,128)(2,1)S(1)} %get-tuple-element.96), channel_id=1, source_target_pairs={{0,1},{1,2},{2,3},{4,5},{5,6},{6,7},{8,9},{9,10},{10,11},{12,13},{... | collective-permute-start | bytes 98312 | tf_op jit(solution)/shard_map/ppermute | solution.py:22
  121.3 3.4 %collective-permute-done.5 = bf16[1,128,128]{2,1,0:T(8,128)(2,1)S(1)} collective-permute-done((bf16[1,128,128]{2,1,0:T(8,128)(2,1)S(1)}, bf16[1,128,128]{2,1,0:T(8,128)(2,1)S(1)}, u32[]{:S(2)}, u32[]{:S(2)}) %collective-permute-start.5) | collective-permute-done | bytes 32800 | tf_op jit(solution)/shard_map/ppermute | solution.py:23
  132.0 3.5 %collective-permute-start.8 = (bf16[1,128,256]{2,1,0:T(8,128)(2,1)S(1)}, bf16[1,128,256]{2,1,0:T(8,128)(2,1)S(1)}, u32[]{:S(2)}, u32[]{:S(2)}) collective-permute-start(bf16[1,128,256]{2,1,0:T(8,128)(2,1)S(1)} %get-tuple-element.70), channel_id=1, source_target_pairs={{0,1},{1,2},{2,3},{4,5},{5,6},{6,7},{8,9},{9,10},{10,11},{12,13},{... | collective-permute-start | bytes 196616 | tf_op jit(solution)/shard_map/ppermute | solution.py:22
  135.5 1.5 collective-permute-start.9
  137.4 4.3 %collective-permute-done.9 = bf16[1,128,256]{2,1,0:T(8,128)(2,1)S(1)} collective-permute-done((bf16[1,128,256]{2,1,0:T(8,128)(2,1)S(1)}, bf16[1,128,256]{2,1,0:T(8,128)(2,1)S(1)}, u32[]{:S(2)}, u32[]{:S(2)}) %collective-permute-start.9) | collective-permute-done | bytes 65568 | tf_op jit(solution)/shard_map/ppermute | solution.py:23
  142.2 1.7 fusion.153
  143.9 1.6 copy.98
  145.5 2.4 fusion.165
  148.7 2.3 fusion.166
  151.0 1.7 copy.97
  152.7 2.4 multiply_convert_fusion
  159.1 3.5 %collective-permute-start.10 = (bf16[1,128,128]{2,1,0:T(8,128)(2,1)S(1)}, bf16[1,128,128]{2,1,0:T(8,128)(2,1)S(1)}, u32[]{:S(2)}, u32[]{:S(2)}) collective-permute-start(bf16[1,128,128]{2,1,0:T(8,128)(2,1)S(1)} %get-tuple-element.94), channel_id=1, source_target_pairs={{0,1},{1,2},{2,3},{4,5},{5,6},{6,7},{8,9},{9,10},{10,11},{12,13},{... | collective-permute-start | bytes 98312 | tf_op jit(solution)/shard_map/ppermute | solution.py:22
  165.0 3.4 %collective-permute-done.11 = bf16[1,128,128]{2,1,0:T(8,128)(2,1)S(1)} collective-permute-done((bf16[1,128,128]{2,1,0:T(8,128)(2,1)S(1)}, bf16[1,128,128]{2,1,0:T(8,128)(2,1)S(1)}, u32[]{:S(2)}, u32[]{:S(2)}) %collective-permute-start.11) | collective-permute-done | bytes 32800 | tf_op jit(solution)/shard_map/ppermute | solution.py:23
  174.0 1.9 collective-permute-start.12
  178.1 3.6 %collective-permute-done.13 = bf16[1,128,128]{2,1,0:T(8,128)(2,1)S(1)} collective-permute-done((bf16[1,128,128]{2,1,0:T(8,128)(2,1)S(1)}, bf16[1,128,128]{2,1,0:T(8,128)(2,1)S(1)}, u32[]{:S(2)}, u32[]{:S(2)}) %collective-permute-start.13) | collective-permute-done | bytes 32800 | tf_op jit(solution)/shard_map/ppermute | solution.py:23
  186.0 85.7 %all-reduce.32.cloned.1.call-done = (f32[162,128]{1,0:T(8,128)}, f32[3,3,128,128]{3,2,1,0:T(8,128)}, f32[3,3,256,128]{3,2,1,0:T(8,128)}) async-done(((f32[162,128]{1,0:T(8,128)}, f32[3,3,128,128]{3,2,1,0:T(8,128)}, f32[3,3,256,128]{3,2,1,0:T(8,128)}), (f32[162,128]{1,0:T(8,128)}, f32[3,3,128,128]{3,2,1,0:T(8,128)}, f32[3,3,256,128]{3,2,1,0:T(8,128)})) %all-reduce.32.cloned.1.call-update) | async-done | bytes 1852432 | tf_op jit(solution)/shard_map/psum | solution.py:11
  273.5 19.2 %all-reduce.25 = (f32[1]{0:T(128)}, f32[128]{0:T(128)S(1)}, f32[128]{0:T(128)S(1)}, f32[7,7,2,128]{3,2,1,0:T(2,128)S(1)}, f32[128]{0:T(128)S(1)}, /*index=5*/f32...) all-reduce(f32[1]{0:T(128)} %bitcast.60, ...), channel_id=1, replica_groups=mesh['groups'=2,'tm'=4,'space'=4] {'space'}, use_global_device_ids=true, to_apply=%region_1.2 | all-reduce | flops 13315 | bytes 106520 | tf_op jit(solution)/shard_map/psum | solution.py:11
  292.7 11.7 %all-reduce.27 = (f32[1]{0:T(128)}, f32[128]{0:T(128)}, f32[128]{0:T(128)}, f32[7,7,2,128]{3,2,1,0:T(2,128)}, f32[128]{0:T(128)}, /*index=5*/f32[128]{0:T(128)}, f32[128,2]{0,1:T(2,128)}, f32[2]{0:T(128)}) all-reduce(f32[1]{0:T(128)} %get-tuple-element.12, ...), channel_id=1, replica_groups=mesh['groups'=2,'tm'=4,'space'=4] {'tm'}, use_global_device_ids=true, to_apply=%region_2.3 | all-reduce | flops 13315 | bytes 106520 | tf_op jit(solution)/shard_map/psum | solution.py:11
  304.4 17.2 %all-reduce.34.cloned.1.call-done = (f32[162,128]{1,0:T(8,128)}, f32[3,3,128,128]{3,2,1,0:T(8,128)}, f32[3,3,256,128]{3,2,1,0:T(8,128)}) async-done(((f32[162,128]{1,0:T(8,128)}, f32[3,3,128,128]{3,2,1,0:T(8,128)}, f32[3,3,256,128]{3,2,1,0:T(8,128)}), (f32[162,128]{1,0:T(8,128)}, f32[3,3,128,128]{3,2,1,0:T(8,128)}, f32[3,3,256,128]{3,2,1,0:T(8,128)})) %all-reduce.34.cloned.1.call-update) | async-done | bytes 1852432 | tf_op jit(solution)/shard_map/psum | solution.py:11
  321.6 1.6 copy.332
  323.3 1.9 copy.333
  (401 shorter events, 110.5 us)
Async XLA Ops:
  7.2 105.9 %copy-start = (bf16[162,128]{1,0:T(8,128)(2,1)S(1)}, bf16[162,128]{1,0:T(8,128)(2,1)}, u32[]{:S(2)}) copy-start(bf16[162,128]{1,0:T(8,128)(2,1)} %param.18) | copy-start | bytes 124420
  7.2 16.8 %copy-start.5 = (bf16[3,3,256,128]{3,2,1,0:T(8,128)(2,1)S(1)}, bf16[3,3,256,128]{3,2,1,0:T(8,128)(2,1)}, u32[]{:S(2)}) copy-start(bf16[3,3,256,128]{3,2,1,0:T(8,128)(2,1)} %param.24) | copy-start | bytes 1769476
  7.2 17.6 %copy-start.8 = (bf16[3,3,128,128]{3,2,1,0:T(8,128)(2,1)S(1)}, bf16[3,3,128,128]{3,2,1,0:T(8,128)(2,1)}, u32[]{:S(2)}) copy-start(bf16[3,3,128,128]{3,2,1,0:T(8,128)(2,1)} %param.20) | copy-start | bytes 884740
  7.2 264.5 %all-reduce.32.cloned.1.call-start = ((), (), s32[]{:S(2)}) async-start(), calls=%async_computation | async-start | bytes 3710976 | tf_op jit(solution)/shard_map/psum | solution.py:11
  8.4 20.4 %collective-permute-start = (bf16[4,128,256]{2,1,0:T(8,128)(2,1)S(1)}, bf16[4,128,256]{2,1,0:T(8,128)(2,1)S(1)}, u32[]{:S(2)}, u32[]{:S(2)}) collective-permute-start(bf16[4,128,256]{2,1,0:T(8,128)(2,1)S(1)} %get-tuple-element.72), channel_id=1, source_target_pairs={{0,1},{1,2},{2,3},{4,5},{5,6},{6,7},{8,9},{9,10},{10,11},{12,13},{... | collective-permute-start | bytes 786440 | tf_op jit(solution)/shard_map/ppermute | solution.py:22
  13.4 15.5 %collective-permute-start.1 = (bf16[4,128,256]{2,1,0:T(8,128)(2,1)S(1)}, bf16[4,128,256]{2,1,0:T(8,128)(2,1)S(1)}, u32[]{:S(2)}, u32[]{:S(2)}) collective-permute-start(bf16[4,128,256]{2,1,0:T(8,128)(2,1)S(1)} %get-tuple-element.73), channel_id=1, source_target_pairs={{1,0},{2,1},{3,2},{5,4},{6,5},{7,6},{9,8},{10,9},{11,10},{13,12},{... | collective-permute-start | bytes 786440 | tf_op jit(solution)/shard_map/ppermute | solution.py:23
  15.4 12.1 %collective-permute-start.6 = (bf16[2,3,128]{2,1,0:T(4,128)(2,1)S(1)}, bf16[2,3,128]{2,1,0:T(4,128)(2,1)S(1)}, u32[]{:S(2)}, u32[]{:S(2)}) collective-permute-start(bf16[2,3,128]{2,1,0:T(4,128)(2,1)S(1)} %get-tuple-element.197), channel_id=1, source_target_pairs={{0,1},{1,2},{2,3},{4,5},{5,6},{6,7},{8,9},{9,10},{10,11},{12,13},{... | collective-permute-start | bytes 4616 | tf_op jit(solution)/shard_map/ppermute | solution.py:22
  20.0 7.6 %collective-permute-start.7 = (bf16[2,3,128]{2,1,0:T(4,128)(2,1)S(1)}, bf16[2,3,128]{2,1,0:T(4,128)(2,1)S(1)}, u32[]{:S(2)}, u32[]{:S(2)}) collective-permute-start(bf16[2,3,128]{2,1,0:T(4,128)(2,1)S(1)} %get-tuple-element.198), channel_id=1, source_target_pairs={{1,0},{2,1},{3,2},{5,4},{6,5},{7,6},{9,8},{10,9},{11,10},{13,12},{... | collective-permute-start | bytes 4616 | tf_op jit(solution)/shard_map/ppermute | solution.py:23
  22.0 4.2 %copy-start.51 = (s32[1,2,8,128]{3,2,1,0:T(8,128)S(1)}, s32[1,2,8,128]{3,2,1,0:T(8,128)}, u32[]{:S(2)}) copy-start(s32[1,2,8,128]{3,2,1,0:T(8,128)} %param.17) | copy-start | bytes 24580
  22.0 4.9 %copy-start.50 = (bf16[7,7,2,128]{3,2,1,0:T(2,128)(2,1)S(1)}, bf16[7,7,2,128]{3,2,1,0:T(2,128)(2,1)}, u32[]{:S(2)}) copy-start(bf16[7,7,2,128]{3,2,1,0:T(2,128)(2,1)} %param.22) | copy-start | bytes 75268
  22.0 5.6 %copy-start.44 = (bf16[1,2,8,128]{3,2,1,0:T(8,128)(2,1)S(1)}, bf16[1,2,8,128]{3,2,1,0:T(8,128)(2,1)}, u32[]{:S(2)}) copy-start(bf16[1,2,8,128]{3,2,1,0:T(8,128)(2,1)} %param.16) | copy-start | bytes 12292
  24.0 4.9 %copy-start.6 = (bf16[1,8,128,256]{3,2,1,0:T(8,128)(2,1)S(1)}, bf16[1,8,128,256]{3,2,1,0:T(8,128)(2,1)}, u32[]{:S(2)}) copy-start(bf16[1,8,128,256]{3,2,1,0:T(8,128)(2,1)} %param.14) | copy-start | bytes 1572868
  29.9 6.5 %collective-permute-start.3 = (bf16[16,128,256]{2,1,0:T(8,128)(2,1)}, bf16[16,128,256]{2,1,0:T(8,128)(2,1)S(1)}, u32[]{:S(2)}, u32[]{:S(2)}) collective-permute-start(bf16[16,128,256]{2,1,0:T(8,128)(2,1)} %pad_maximum_fusion.2), channel_id=1, source_target_pairs={{4,0},{8,4},{12,8},{5,1},{9,5},{13,9},{6,2},{10,6},{14,10},{7,3},{... | collective-permute-start | bytes 3145736 | tf_op jit(solution)/shard_map/ppermute | solution.py:31
  32.2 37.7 %collective-permute-start.2 = (bf16[16,128,256]{2,1,0:T(8,128)(2,1)}, bf16[16,128,256]{2,1,0:T(8,128)(2,1)}, u32[]{:S(2)}, u32[]{:S(2)}) collective-permute-start(bf16[16,128,256]{2,1,0:T(8,128)(2,1)} %pad_maximum_fusion.2), channel_id=1, source_target_pairs={{0,4},{4,8},{8,12},{1,5},{5,9},{9,13},{2,6},{6,10},{10,14},{3,7},{... | collective-permute-start | bytes 3145736 | tf_op jit(solution)/shard_map/ppermute | solution.py:31
  110.9 1.6 copy-start.31
  110.9 1.6 copy-start.32
  113.1 7.1 %copy-start.49 = (bf16[98,128]{1,0:T(8,128)(2,1)S(1)}, bf16[98,128]{1,0:T(8,128)(2,1)}, u32[]{:S(2)}) copy-start(bf16[98,128]{1,0:T(8,128)(2,1)} %reshape.316) | copy-start | bytes 75268
  113.1 7.1 %copy-start.54 = (f32[128]{0:T(128)S(1)}, f32[128]{0:T(128)}, u32[]{:S(2)}) copy-start(f32[128]{0:T(128)} %param.23) | copy-start | bytes 1540
  114.4 7.0 %collective-permute-start.4 = (bf16[1,128,128]{2,1,0:T(8,128)(2,1)S(1)}, bf16[1,128,128]{2,1,0:T(8,128)(2,1)S(1)}, u32[]{:S(2)}, u32[]{:S(2)}) collective-permute-start(bf16[1,128,128]{2,1,0:T(8,128)(2,1)S(1)} %get-tuple-element.96), channel_id=1, source_target_pairs={{0,1},{1,2},{2,3},{4,5},{5,6},{6,7},{8,9},{9,10},{10,11},{12,13},{... | collective-permute-start | bytes 98312 | tf_op jit(solution)/shard_map/ppermute | solution.py:22
  118.9 5.8 %collective-permute-start.5 = (bf16[1,128,128]{2,1,0:T(8,128)(2,1)S(1)}, bf16[1,128,128]{2,1,0:T(8,128)(2,1)S(1)}, u32[]{:S(2)}, u32[]{:S(2)}) collective-permute-start(bf16[1,128,128]{2,1,0:T(8,128)(2,1)S(1)} %get-tuple-element.97), channel_id=1, source_target_pairs={{1,0},{2,1},{3,2},{5,4},{6,5},{7,6},{9,8},{10,9},{11,10},{13,12},{... | collective-permute-start | bytes 98312 | tf_op jit(solution)/shard_map/ppermute | solution.py:23
  132.0 5.4 %collective-permute-start.8 = (bf16[1,128,256]{2,1,0:T(8,128)(2,1)S(1)}, bf16[1,128,256]{2,1,0:T(8,128)(2,1)S(1)}, u32[]{:S(2)}, u32[]{:S(2)}) collective-permute-start(bf16[1,128,256]{2,1,0:T(8,128)(2,1)S(1)} %get-tuple-element.70), channel_id=1, source_target_pairs={{0,1},{1,2},{2,3},{4,5},{5,6},{6,7},{8,9},{9,10},{10,11},{12,13},{... | collective-permute-start | bytes 196616 | tf_op jit(solution)/shard_map/ppermute | solution.py:22
  135.5 6.2 %collective-permute-start.9 = (bf16[1,128,256]{2,1,0:T(8,128)(2,1)S(1)}, bf16[1,128,256]{2,1,0:T(8,128)(2,1)S(1)}, u32[]{:S(2)}, u32[]{:S(2)}) collective-permute-start(bf16[1,128,256]{2,1,0:T(8,128)(2,1)S(1)} %get-tuple-element.71), channel_id=1, source_target_pairs={{1,0},{2,1},{3,2},{5,4},{6,5},{7,6},{9,8},{10,9},{11,10},{13,12},{... | collective-permute-start | bytes 196616 | tf_op jit(solution)/shard_map/ppermute | solution.py:23
  151.0 1.7 copy-start.56
  152.7 2.4 copy-start.57
  152.7 2.4 copy-start.58
  159.1 5.9 %collective-permute-start.10 = (bf16[1,128,128]{2,1,0:T(8,128)(2,1)S(1)}, bf16[1,128,128]{2,1,0:T(8,128)(2,1)S(1)}, u32[]{:S(2)}, u32[]{:S(2)}) collective-permute-start(bf16[1,128,128]{2,1,0:T(8,128)(2,1)S(1)} %get-tuple-element.94), channel_id=1, source_target_pairs={{0,1},{1,2},{2,3},{4,5},{5,6},{6,7},{8,9},{9,10},{10,11},{12,13},{... | collective-permute-start | bytes 98312 | tf_op jit(solution)/shard_map/ppermute | solution.py:22
  162.6 5.8 %collective-permute-start.11 = (bf16[1,128,128]{2,1,0:T(8,128)(2,1)S(1)}, bf16[1,128,128]{2,1,0:T(8,128)(2,1)S(1)}, u32[]{:S(2)}, u32[]{:S(2)}) collective-permute-start(bf16[1,128,128]{2,1,0:T(8,128)(2,1)S(1)} %get-tuple-element.95), channel_id=1, source_target_pairs={{1,0},{2,1},{3,2},{5,4},{6,5},{7,6},{9,8},{10,9},{11,10},{13,12},{... | collective-permute-start | bytes 98312 | tf_op jit(solution)/shard_map/ppermute | solution.py:23
  174.0 4.1 %collective-permute-start.12 = (bf16[1,128,128]{2,1,0:T(8,128)(2,1)S(1)}, bf16[1,128,128]{2,1,0:T(8,128)(2,1)S(1)}, u32[]{:S(2)}, u32[]{:S(2)}) collective-permute-start(bf16[1,128,128]{2,1,0:T(8,128)(2,1)S(1)} %get-tuple-element.92), channel_id=1, source_target_pairs={{0,1},{1,2},{2,3},{4,5},{5,6},{6,7},{8,9},{9,10},{10,11},{12,13},{... | collective-permute-start | bytes 98312 | tf_op jit(solution)/shard_map/ppermute | solution.py:22
  176.0 5.8 %collective-permute-start.13 = (bf16[1,128,128]{2,1,0:T(8,128)(2,1)S(1)}, bf16[1,128,128]{2,1,0:T(8,128)(2,1)S(1)}, u32[]{:S(2)}, u32[]{:S(2)}) collective-permute-start(bf16[1,128,128]{2,1,0:T(8,128)(2,1)S(1)} %get-tuple-element.93), channel_id=1, source_target_pairs={{1,0},{2,1},{3,2},{5,4},{6,5},{7,6},{9,8},{10,9},{11,10},{13,12},{... | collective-permute-start | bytes 98312 | tf_op jit(solution)/shard_map/ppermute | solution.py:23
  186.0 87.1 %copy-start.22 = (bf16[1024,128]{1,0:T(8,128)(2,1)S(1)}, bf16[1024,128]{1,0:T(8,128)(2,1)}, u32[]{:S(2)}) copy-start(bf16[1024,128]{1,0:T(8,128)(2,1)} %copy-done.21) | copy-start | bytes 786436
  186.0 135.6 %all-reduce.34.cloned.1.call-start = ((), (), s32[]{:S(2)}) async-start(), calls=%async_computation.1 | async-start | bytes 3710976 | tf_op jit(solution)/shard_map/psum | solution.py:11
  321.6 3.5 %copy-start.7 = (f32[3,3,256,128]{3,2,1,0:T(8,128)S(1)}, f32[3,3,256,128]{3,2,1,0:T(8,128)}, u32[]{:S(2)}) copy-start(f32[3,3,256,128]{3,2,1,0:T(8,128)} %get-tuple-element.320) | copy-start | bytes 3538948
  (44 other events, 47.5 us)
Sparse Core Ops, SparseCore 0:
  186.1 85.5 all-reduce.31
  274.3 47.2 all-reduce.33
